TPU v7x, 32 devices: a whole 2x2x4 slice. The times are simulated.
32 devices in a mesh: doc: 8 (over y, x, core), seq: 4 (over z).
Axes of the slice: x: 2, y: 2, z: 4, core: 2. Of those that a mesh axis runs over, the one named last changes fastest.
Arguments:
- images: bfloat16 [8, 4, 128, 8192], P('doc', None, None, 'seq'), may hold values from -6 to 6
- kv_weight: bfloat16 [1024, 8192], P('doc', 'seq'), may hold values from -0.0625 to 0.0625
- q_gain: float32 [128], replicated, may hold values from 0.1 to 1.9
- k_gain: float32 [128], replicated, may hold values from 0.1 to 1.9
- queries: bfloat16 [8, 512, 4096], P('doc', 'seq'), may hold values from -6 to 6
- cotangent: bfloat16 [8, 512, 4096], P('doc', 'seq'), may hold values from -6 to 6
- tile_count: int32 [8], replicated, may hold values from 1 to 4, as said below
- tile_target: int32 [8, 4], replicated, may hold values from 0 to 8, as said below
- tile_source: int32 [8, 4], replicated, may hold values from 0 to 8, as said below
- text_length: int32 [8], replicated, may hold values from 64 to 512, as said below
Outputs:
- attn_out: bfloat16 [8, 512, 4096], P('doc', 'seq')
- kv_weight_grad: float32 [1024, 8192], P('doc', 'seq')
Inputs may be any that keep to these rules, and one draw needn't show every extreme that they name: `tile_count`: some document has 4 tiles and some has 1. `tile_target`: 8 marks an empty slot. The tile in slot k of an encoder device is tile k of its document; no encoder device holds two tiles of one document. Agrees with tile_source and tile_count. `tile_source`: 8 for k at or beyond the document's tile count; otherwise the encoder device that holds tile k in its slot k. `text_length`: live rows come first; some document has all 512 rows live.
All inputs are finite; a program needn't handle non-finite values.
Results may differ from a plain program's by a relative error of at most 0.03.
Values may be sent and summed in bfloat16 or wider, within the bound.
No kernel may reach another device: no remote copies, remote signals or barrier semaphores. Data moves between devices by JAX's collectives and lax.ppermute only.
A program may use at most 64 MiB of HBM per device.

v0:
```python
import math
import jax
import jax.numpy as jnp
from jax import lax
from jax.sharding import PartitionSpec as P

EPS = 1e-05


def cross_core(kv_tiles, query_rows, grad_rows, q_gain, k_gain, key_live, row_live):
    key_width = kv_tiles.shape[-1] // 2
    head_dim = q_gain.shape[0]
    kv_heads = key_width // head_dim
    token_rows = query_rows.shape[0]
    q_heads = query_rows.shape[1] // head_dim
    group_size = q_heads // kv_heads
    inv_root = 1.0 / math.sqrt(head_dim)
    key_raw = kv_tiles[:, :key_width].reshape(-1, kv_heads, head_dim).astype(jnp.float32)
    values = kv_tiles[:, key_width:].reshape(-1, kv_heads, head_dim)
    key_scale = lax.rsqrt(jnp.mean(key_raw * key_raw, axis=-1, keepdims=True) + EPS)
    key_normed = (key_raw * key_scale * k_gain).astype(jnp.bfloat16)
    query_raw = query_rows.reshape(token_rows, kv_heads, group_size, head_dim).astype(jnp.float32)
    query_scale = lax.rsqrt(jnp.mean(query_raw * query_raw, axis=-1, keepdims=True) + EPS)
    query_normed = (query_raw * query_scale * q_gain).astype(jnp.bfloat16)
    row_mask = row_live[:, None, None, None]
    grad_live = grad_rows.reshape(token_rows, kv_heads, group_size, head_dim) * row_mask.astype(
        jnp.bfloat16
    )

    def one_head(items):
        key_head, value_head, query_head, grad_head = items
        scores = (
            jnp.einsum("tgd,ld->tgl", query_head, key_head, preferred_element_type=jnp.float32)
            * inv_root
        )
        expd = jnp.exp(scores) * key_live
        attend = expd / jnp.sum(expd, axis=-1, keepdims=True)
        attend_low = attend.astype(jnp.bfloat16)
        mixed = jnp.einsum(
            "tgl,ld->tgd", attend_low, value_head, preferred_element_type=jnp.float32
        )
        mixed_low = (mixed * row_live[:, None, None]).astype(jnp.bfloat16)
        grad_attend = jnp.einsum(
            "tgd,ld->tgl", grad_head, value_head, preferred_element_type=jnp.float32
        )
        grad_scores = attend * (grad_attend - jnp.sum(attend * grad_attend, axis=-1, keepdims=True))
        grad_low = (grad_scores * inv_root).astype(jnp.bfloat16)
        grad_keyn = jnp.einsum(
            "tgl,tgd->ld", grad_low, query_head, preferred_element_type=jnp.float32
        )
        grad_values = jnp.einsum(
            "tgl,tgd->ld", attend_low, grad_head, preferred_element_type=jnp.float32
        )
        return (mixed_low, grad_keyn, grad_values)

    head_items = (
        jnp.moveaxis(key_normed, 1, 0),
        jnp.moveaxis(values, 1, 0),
        jnp.moveaxis(query_normed, 1, 0),
        jnp.moveaxis(grad_live, 1, 0),
    )
    mixed_heads, keyn_heads, value_heads = lax.map(one_head, head_items)
    attn_rows = jnp.moveaxis(mixed_heads, 0, 1).reshape(token_rows, -1)
    grad_keyn = jnp.moveaxis(keyn_heads, 0, 1)
    grad_values = jnp.moveaxis(value_heads, 0, 1)
    weighted = grad_keyn * k_gain
    cubed = key_scale * key_scale * key_scale
    grad_keys = key_scale * weighted - key_raw * cubed * jnp.mean(
        weighted * key_raw, axis=-1, keepdims=True
    )
    grad_kv = jnp.concatenate(
        [grad_keys.reshape(-1, key_width), grad_values.reshape(-1, key_width)], axis=-1
    )
    return (attn_rows, grad_kv)


def per_device(
    images,
    kv_weight,
    q_gain,
    k_gain,
    queries,
    cotangent,
    tile_count,
    tile_target,
    tile_source,
    text_length,
):
    n_doc = lax.axis_size("doc")
    n_seq = lax.axis_size("seq")
    doc_at = lax.axis_index("doc")
    seq_at = lax.axis_index("seq")
    slots = images.shape[1]
    tile_rows = images.shape[2]
    part_rows = tile_rows // n_seq
    own_cols = images[0].reshape(slots * tile_rows, images.shape[3])
    partial_value = lax.dot_general(
        own_cols,
        lax.all_gather(kv_weight, "doc", axis=0, tiled=True),
        (((1,), (1,)), ((), ())),
        preferred_element_type=jnp.float32,
    )
    width = partial_value.shape[1]
    partial_value = partial_value.reshape(slots, tile_rows, width)
    summed = lax.psum(partial_value.astype(jnp.bfloat16), "seq").astype(jnp.float32)
    own_share = lax.dynamic_slice_in_dim(summed, seq_at * part_rows, part_rows, 1)
    kv_own = own_share.astype(jnp.bfloat16)
    doc_ids = jnp.arange(n_doc, dtype=jnp.int32)
    slot_ids = jnp.arange(slots, dtype=jnp.int32)
    targets = tile_target[doc_at]
    send_map = (targets[None, :] == doc_ids[:, None]).astype(jnp.bfloat16)
    outgoing = jnp.einsum(
        "ds,src->drc", send_map, kv_own, preferred_element_type=jnp.float32
    ).astype(jnp.bfloat16)
    incoming = lax.all_to_all(outgoing, "doc", split_axis=0, concat_axis=0, tiled=True)
    tiles_here = tile_count[doc_at]
    sources = tile_source[doc_at]
    live_slot = slot_ids < tiles_here
    pick_map = ((sources[:, None] == doc_ids[None, :]) & live_slot[:, None]).astype(jnp.bfloat16)
    kv_part = jnp.einsum(
        "se,erc->src", pick_map, incoming, preferred_element_type=jnp.float32
    ).astype(jnp.bfloat16)
    kv_full = lax.all_gather(kv_part, "seq", axis=1, tiled=True)
    token_rows = queries.shape[1]
    key_live = (jnp.arange(slots * tile_rows, dtype=jnp.int32) // tile_rows < tiles_here).astype(
        jnp.float32
    )
    row_index = seq_at * token_rows + jnp.arange(token_rows, dtype=jnp.int32)
    row_live = (row_index < text_length[doc_at]).astype(jnp.float32)
    attn_rows, grad_kv = cross_core(
        kv_full.reshape(slots * tile_rows, width),
        queries[0],
        cotangent[0],
        q_gain,
        k_gain,
        key_live,
        row_live,
    )
    attn_out = attn_rows[None]
    grad_kv = grad_kv.reshape(slots, tile_rows, width)
    grad_sum = lax.psum(grad_kv.astype(jnp.bfloat16), "seq").astype(jnp.float32)
    grad_share = lax.dynamic_slice_in_dim(grad_sum, seq_at * part_rows, part_rows, 1)
    grad_own = grad_share.astype(jnp.bfloat16)
    back_out = jnp.einsum(
        "se,src->erc", pick_map, grad_own, preferred_element_type=jnp.float32
    ).astype(jnp.bfloat16)
    back_in = lax.all_to_all(back_out, "doc", split_axis=0, concat_axis=0, tiled=True)
    returned = jnp.einsum(
        "ds,drc->src", send_map, back_in, preferred_element_type=jnp.float32
    ).astype(jnp.bfloat16)
    grad_full = lax.all_gather(returned, "seq", axis=1, tiled=True)
    grad_flat = grad_full.reshape(slots * tile_rows, width)
    rows_each = width // n_doc
    weight_part = lax.dot_general(
        grad_flat, own_cols, (((0,), (0,)), ((), ())), preferred_element_type=jnp.float32
    )
    weight_sum = lax.psum(weight_part.astype(jnp.bfloat16), "doc").astype(jnp.float32)
    weight_grad = lax.dynamic_slice_in_dim(weight_sum, doc_at * rows_each, rows_each, 0)
    return (attn_out, weight_grad)


def solution(mesh):
    return jax.shard_map(
        per_device,
        mesh=mesh,
        in_specs=(
            P("doc", None, None, "seq"),
            P("doc", "seq"),
            P(),
            P(),
            P("doc", "seq", None),
            P("doc", "seq", None),
            P(),
            P(),
            P(),
            P(),
        ),
        out_specs=(P("doc", "seq", None), P("doc", "seq")),
        check_vma=False,
    )
```

profile of v0, /device:TPU:0, one launch (start us, length us, event | category | flops | bytes accessed | tf_op | source)
XLA Modules:
  0.0 441.7 jit_solution(6251067855293527332)
XLA Ops:
  8.0 41.2 %all-gather.4.cloned.1.call-done = bf16[1024,2048]{1,0:T(8,128)(2,1)} async-done(((bf16[128,2048]{1,0:T(8,128)(2,1)}), bf16[1024,2048]{1,0:T(8,128)(2,1)}) %all-gather.4.cloned.1.call-update) | async-done | bytes 4194320 | tf_op jit(solution)/shard_map/all_gather | solution.py:99
  49.2 5.5 %fusion.64 = bf16[4,128,1024]{2,1,0:T(8,128)(2,1)} fusion(bf16[1024,2048]{1,0:T(8,128)(2,1)} %all-gather.4.cloned.1.call-done, bf16[1,4,128,2048]{3,2,1,0:T(8,128)(2,1)S(1)} %copy-done), kind=kOutput, calls=%fused_computation.63 | convolution fusion | flops 2148007936 | bytes 7340032 | tf_op jit(solution)/shard_map/dot_general | solution.py:97
  55.0 51.8 %all-reduce.4.cloned.1.call-done = bf16[4,128,1024]{2,1,0:T(8,128)(2,1)} async-done(((bf16[4,128,1024]{2,1,0:T(8,128)(2,1)}), bf16[4,128,1024]{2,1,0:T(8,128)(2,1)}) %all-reduce.4.cloned.1.call-update) | async-done | bytes 1048592 | tf_op jit(solution)/shard_map/psum | solution.py:105
  109.3 3.7 all-to-all-start
  114.5 8.2 %all-to-all-done = bf16[8,32,1024]{2,1,0:T(8,128)(2,1)S(1)} async-done(((bf16[8,32,1024]{2,1,0:T(8,128)(2,1)}), bf16[8,32,1024]{2,1,0:T(8,128)(2,1)S(1)}, u32[]{:S(2)}, u32[]{:S(2)}) %all-to-all-start) | async-done | bytes 524320 | tf_op jit(solution)/shard_map/all_to_all | solution.py:115
  124.8 2.3 copy.40
  127.0 1.6 copy.33
  129.6 2.3 multiply_bitcast_fusion
  131.9 1.4 fusion.69
  133.3 16.2 %all-gather.6.cloned.1.call-done = bf16[4,128,1024]{2,0,1:T(4,128)(2,1)} async-done(((bf16[4,32,1024]{2,0,1:T(4,128)(2,1)}), bf16[4,128,1024]{2,0,1:T(4,128)(2,1)}) %all-gather.6.cloned.1.call-update) | async-done | bytes 1048592 | tf_op jit(solution)/shard_map/all_gather | solution.py:123
  149.5 1.5 copy.37
  151.0 1.3 fusion.89
  152.3 1.6 copy.38
  154.0 2.1 copy.39
  157.1 87.8 %while.15 = (s32[]{:T(128)}, bf16[4,128,8,128]{3,1,2,0:T(8,128)(2,1)}, f32[4,512,128]{1,2,0:T(8,128)}, bf16[4,512,128]{2,1,0:T(8,128)(2,1)}, bf16[4,128,8,128]{1...) while((s32[]{:T(128)}, ...), condition=%wide.region_6.7_spmd.clone, body=%wide.region_3.6_spmd.clone.sunk | while | flops 682891136 | bytes 27433116 | solution.py:62
  157.7 2.8 fusion.115
  160.5 2.7 fusion.117
  163.2 9.8 %fusion.118 = f32[4,512,128]{1,2,0:T(8,128)} fusion(f32[4,512,128]{1,2,0:T(8,128)} %get-tuple-element.222, s32[]{:T(128)} %get-tuple-element.220, f32[128,8,512]{2,0,1:T(8,128)} %fusion.117, bf16[4,128,8,128]{1,3,2,0:T(8,128)(2,1)} %get-tuple-element.236, f32[128,8,512]{2,0,1:T(8,128)} %get-tuple-element.206, f32[128,8]{0,1:T(8,128)S(1)} %get-tuple-element.207, ...), kind=kOutput, calls=%fused_computation.13.clone.1 | convolution fusion | flops 139986432 | bytes 8926208 | tf_op jit(solution)/shard_map/while/body/eval_jaxpr/tgl,tgd->ld/dot_general | solution.py:48
  173.0 3.1 fusion.119
  176.8 2.2 fusion.116
  179.6 2.8 fusion.115
  182.4 2.7 fusion.117
  185.2 9.8 %fusion.118 = f32[4,512,128]{1,2,0:T(8,128)} fusion(f32[4,512,128]{1,2,0:T(8,128)} %get-tuple-element.222, s32[]{:T(128)} %get-tuple-element.220, f32[128,8,512]{2,0,1:T(8,128)} %fusion.117, bf16[4,128,8,128]{1,3,2,0:T(8,128)(2,1)} %get-tuple-element.236, f32[128,8,512]{2,0,1:T(8,128)} %get-tuple-element.206, f32[128,8]{0,1:T(8,128)S(1)} %get-tuple-element.207, ...), kind=kOutput, calls=%fused_computation.13.clone.1 | convolution fusion | flops 139986432 | bytes 8926208 | tf_op jit(solution)/shard_map/while/body/eval_jaxpr/tgl,tgd->ld/dot_general | solution.py:48
  195.0 3.1 fusion.119
  198.7 2.2 fusion.116
  201.6 2.8 fusion.115
  204.4 2.7 fusion.117
  207.1 9.8 %fusion.118 = f32[4,512,128]{1,2,0:T(8,128)} fusion(f32[4,512,128]{1,2,0:T(8,128)} %get-tuple-element.222, s32[]{:T(128)} %get-tuple-element.220, f32[128,8,512]{2,0,1:T(8,128)} %fusion.117, bf16[4,128,8,128]{1,3,2,0:T(8,128)(2,1)} %get-tuple-element.236, f32[128,8,512]{2,0,1:T(8,128)} %get-tuple-element.206, f32[128,8]{0,1:T(8,128)S(1)} %get-tuple-element.207, ...), kind=kOutput, calls=%fused_computation.13.clone.1 | convolution fusion | flops 139986432 | bytes 8926208 | tf_op jit(solution)/shard_map/while/body/eval_jaxpr/tgl,tgd->ld/dot_general | solution.py:48
  216.9 3.1 fusion.119
  220.7 2.2 fusion.116
  223.5 2.8 fusion.115
  226.3 2.7 fusion.117
  229.0 9.8 %fusion.118 = f32[4,512,128]{1,2,0:T(8,128)} fusion(f32[4,512,128]{1,2,0:T(8,128)} %get-tuple-element.222, s32[]{:T(128)} %get-tuple-element.220, f32[128,8,512]{2,0,1:T(8,128)} %fusion.117, bf16[4,128,8,128]{1,3,2,0:T(8,128)(2,1)} %get-tuple-element.236, f32[128,8,512]{2,0,1:T(8,128)} %get-tuple-element.206, f32[128,8]{0,1:T(8,128)S(1)} %get-tuple-element.207, ...), kind=kOutput, calls=%fused_computation.13.clone.1 | convolution fusion | flops 139986432 | bytes 8926208 | tf_op jit(solution)/shard_map/while/body/eval_jaxpr/tgl,tgd->ld/dot_general | solution.py:48
  238.9 3.1 fusion.119
  242.6 2.2 fusion.116
  244.8 1.5 fusion.72
  247.5 1.2 reshape.87
  250.9 2.5 pad_maximum_fusion
  253.5 51.4 %all-reduce.6.cloned.1.call-done = bf16[4,128,1024]{2,0,1:T(4,128)(2,1)} async-done(((bf16[4,128,1024]{2,0,1:T(4,128)(2,1)}), bf16[4,128,1024]{2,0,1:T(4,128)(2,1)}) %all-reduce.6.cloned.1.call-update) | async-done | bytes 1048592 | tf_op jit(solution)/shard_map/psum | solution.py:141
  304.9 1.4 convolution_convert_fusion.1
  306.5 13.2 %all_to_all.10 = bf16[8,32,1024]{2,1,0:T(8,128)(2,1)S(1)} all-to-all(bf16[8,32,1024]{2,1,0:T(8,128)(2,1)S(1)} %copy.51), channel_id=1, replica_groups=mesh['doc'=8,'seq'=4] {'doc'}, dimensions={0} | all-to-all | bytes 1048576 | tf_op jit(solution)/shard_map/all_to_all | solution.py:147
  321.1 25.3 %all-gather.8.cloned.1.call-done = bf16[4,128,1024]{2,0,1:T(4,128)(2,1)} async-done(((bf16[4,32,1024]{2,0,1:T(4,128)(2,1)}), bf16[4,128,1024]{2,0,1:T(4,128)(2,1)}) %all-gather.8.cloned.1.call-update) | async-done | bytes 1048592 | tf_op jit(solution)/shard_map/all_gather | solution.py:151
  346.5 1.5 copy.53
  348.0 4.4 convolution_convert_fusion
  352.4 1.9 copy.45
  354.3 1.3 broadcast_in_dim_reshape.3
  355.6 77.2 %all-reduce.8.cloned.1.call-done = bf16[1024,2048]{1,0:T(8,128)(2,1)} async-done(((bf16[1024,2048]{1,0:T(8,128)(2,1)}), bf16[1024,2048]{1,0:T(8,128)(2,1)}) %all-reduce.8.cloned.1.call-update) | async-done | bytes 4194320 | tf_op jit(solution)/shard_map/psum | solution.py:157
  432.7 2.1 dynamic-slice_convert_fusion
  (72 shorter events, 19.1 us)
Async XLA Ops:
  7.2 42.1 %copy-start = (bf16[1,4,128,2048]{3,2,1,0:T(8,128)(2,1)S(1)}, bf16[1,4,128,2048]{3,2,1,0:T(8,128)(2,1)}, u32[]{:S(2)}) copy-start(bf16[1,4,128,2048]{3,2,1,0:T(8,128)(2,1)} %param.12) | copy-start | bytes 6291460
  7.2 42.0 %all-gather.4.cloned.1.call-start = ((), (), s32[]{:S(2)}) async-start(), calls=%async_computation.2 | async-start | bytes 4718592 | tf_op jit(solution)/shard_map/all_gather | solution.py:99
  7.9 46.9 %copy-start.5 = (s32[8,4]{0,1:T(4,128)S(1)}, s32[8,4]{0,1:T(4,128)}, u32[]{:S(2)}) copy-start(s32[8,4]{0,1:T(4,128)} %param.19) | copy-start | bytes 388
  7.9 98.9 %all-reduce.4.cloned.1.call-start = ((), (), s32[]{:S(2)}) async-start(), calls=%async_computation.3 | async-start | bytes 2097152 | tf_op jit(solution)/shard_map/psum | solution.py:105
  54.7 58.3 %copy-start.8 = (s32[8]{0:T(128)S(1)}, s32[8]{0:T(128)}, u32[]{:S(2)}) copy-start(s32[8]{0:T(128)} %param.18) | copy-start | bytes 100
  54.7 58.9 %copy-start.6 = (s32[8,4]{0,1:T(4,128)S(1)}, s32[8,4]{0,1:T(4,128)}, u32[]{:S(2)}) copy-start(s32[8,4]{0,1:T(4,128)} %param.20) | copy-start | bytes 388
  107.8 16.3 %copy-start.9 = (s32[8]{0:T(128)S(1)}, s32[8]{0:T(128)}, u32[]{:S(2)}) copy-start(s32[8]{0:T(128)} %param.21) | copy-start | bytes 100
  109.3 13.4 %all-to-all-start = ((bf16[8,32,1024]{2,1,0:T(8,128)(2,1)}), bf16[8,32,1024]{2,1,0:T(8,128)(2,1)S(1)}, u32[]{:S(2)}, u32[]{:S(2)}) async-start(bf16[8,32,1024]{2,1,0:T(8,128)(2,1)} %copy.35), calls=%async_computation | async-start | bytes 1048576 | tf_op jit(solution)/shard_map/all_to_all | solution.py:115
  113.0 36.5 %all-gather.6.cloned.1.call-start = ((), (), s32[]{:S(2)}) async-start(), calls=%async_computation.4 | async-start | bytes 1310720 | tf_op jit(solution)/shard_map/all_gather | solution.py:123
  123.9 181.0 %all-reduce.6.cloned.1.call-start = ((), (), s32[]{:S(2)}) async-start(), calls=%async_computation.5 | async-start | bytes 2097152 | tf_op jit(solution)/shard_map/psum | solution.py:141
  128.7 3.2 copy-start.7
  152.3 3.8 copy-start.4
  173.0 3.7 copy-start.1
  195.0 3.7 copy-start.1
  216.9 3.7 copy-start.1
  238.9 3.7 copy-start.1
  244.8 1.5 copy-start.2
  247.5 2.4 copy-start.3
  253.4 93.0 %all-gather.8.cloned.1.call-start = ((), (), s32[]{:S(2)}) async-start(), calls=%async_computation.6 | async-start | bytes 1310720 | tf_op jit(solution)/shard_map/all_gather | solution.py:151
  320.9 111.9 %all-reduce.8.cloned.1.call-start = ((), (), s32[]{:S(2)}) async-start(), calls=%async_computation.7 | async-start | bytes 8388608 | tf_op jit(solution)/shard_map/psum | solution.py:157
Sparse Core Ops, SparseCore 0:
  9.9 39.2 all-gather.3
  54.9 51.8 all-reduce.3
  124.0 25.4 all-gather.5
  253.6 51.2 all-reduce.5
  321.0 25.4 all-gather.7
  352.5 80.1 all-reduce.7
where the time goes:
time: 443 us; the launch traced here: 442 us
  waiting for transfers between devices  272 us (61%)
  matrix products  96.6 us (22%)
  other arithmetic  20.8 us (5%)
  local copies, waits for them, and re-layouts  20.3 us (5%)
  between operations  14.3 us (3%)
  blocking collectives  13.2 us (3%)
    psum x1, waiting for transfers between devices, per_device(): lax.psum(weight_part.astype(jnp.bfloat16), 'doc').astype(jnp.float32)  77.2 us
    psum x1, waiting for transfers between devices, per_device(): lax.psum(partial_value.astype(jnp.bfloat16), 'seq').astype(jnp.float32)  51.8 us
    psum x1, waiting for transfers between devices, per_device(): grad_sum = lax.psum(grad_kv.astype(jnp.bfloat16), 'seq').astype(jnp.float32)  51.4 us
    all_gather x1, waiting for transfers between devices, per_device(): lax.all_gather(kv_weight, 'doc', axis=0, tiled=True)  41.2 us
    dot_general x4, matrix products, one_head(): jnp.einsum('tgl,tgd->ld', grad_low, query_head, preferred_element_type=jn...  39.3 us
    all_gather x1, waiting for transfers between devices, per_device(): grad_full = lax.all_gather(returned, 'seq', axis=1, tiled=True)  25.3 us
    all_gather x1, waiting for transfers between devices, per_device(): kv_full = lax.all_gather(kv_part, 'seq', axis=1, tiled=True)  16.2 us
    all_to_all x1, blocking collectives, per_device(): lax.all_to_all(back_out, 'doc', split_axis=0, concat_axis=0, tiled=True)  13.2 us
  transfers between devices with their start and end apart: 7, of which 7 were waited for; matrix products, arithmetic and copies ran while one was open for 3% of the time, Pallas kernels for 0%

commit v1 on v0

--- a/solution.py
+++ b/solution.py
@@ -3,8 +3,14 @@
 import jax.numpy as jnp
 from jax import lax
 from jax.sharding import PartitionSpec as P
+from jax.lax import all_gather
 
 EPS = 1e-05
+
+
+def series_enter(matrix):
+    big = jnp.sum(all_gather(matrix, "seq"), 0)
+    return big
 
 
 def cross_core(kv_tiles, query_rows, grad_rows, q_gain, k_gain, key_live, row_live):
@@ -138,7 +144,7 @@
     )
     attn_out = attn_rows[None]
     grad_kv = grad_kv.reshape(slots, tile_rows, width)
-    grad_sum = lax.psum(grad_kv.astype(jnp.bfloat16), "seq").astype(jnp.float32)
+    grad_sum = series_enter(grad_kv.astype(jnp.bfloat16)).astype(jnp.float32)
     grad_share = lax.dynamic_slice_in_dim(grad_sum, seq_at * part_rows, part_rows, 1)
     grad_own = grad_share.astype(jnp.bfloat16)
     back_out = jnp.einsum(

time: 443 us -> 474 us (1.070)
  waiting for transfers between devices: 272 us -> 300 us
    all_gather x0 -> x1, waiting for transfers between devices: none -> 80.2 us  [series_enter(): big = jnp.sum(all_gather(matrix, 'seq'), 0)]
    psum x1 -> x0, waiting for transfers between devices: 51.4 us -> none  [per_device(): grad_sum = lax.psum(grad_kv.astype(jnp.bfloat16), 'seq').astype(jnp.float32)]
where the time goes in v1:
time: 474 us; the launch traced here: 473 us
  waiting for transfers between devices  300 us (63%)
  matrix products  95.8 us (20%)
  other arithmetic  24.4 us (5%)
  local copies, waits for them, and re-layouts  20.8 us (4%)
  between operations  14.3 us (3%)
  blocking collectives  13.2 us (3%)
    all_gather x1, waiting for transfers between devices, series_enter(): big = jnp.sum(all_gather(matrix, 'seq'), 0)  80.2 us
    psum x1, waiting for transfers between devices, per_device(): lax.psum(weight_part.astype(jnp.bfloat16), 'doc').astype(jnp.float32)  77.2 us
    psum x1, waiting for transfers between devices, per_device(): lax.psum(partial_value.astype(jnp.bfloat16), 'seq').astype(jnp.float32)  51.8 us
    all_gather x1, waiting for transfers between devices, per_device(): lax.all_gather(kv_weight, 'doc', axis=0, tiled=True)  41.2 us
    dot_general x4, matrix products, one_head(): jnp.einsum('tgl,tgd->ld', grad_low, query_head, preferred_element_type=jn...  39.3 us
    all_gather x1, waiting for transfers between devices, per_device(): grad_full = lax.all_gather(returned, 'seq', axis=1, tiled=True)  24.5 us
    all_gather x1, waiting for transfers between devices, per_device(): kv_full = lax.all_gather(kv_part, 'seq', axis=1, tiled=True)  16.1 us
    all_to_all x1, blocking collectives, per_device(): lax.all_to_all(back_out, 'doc', split_axis=0, concat_axis=0, tiled=True)  13.2 us
  transfers between devices with their start and end apart: 7, of which 7 were waited for; matrix products, arithmetic and copies ran while one was open for 3% of the time, Pallas kernels for 0%

profile of v1, /device:TPU:0, one launch (start us, length us, event | category | flops | bytes accessed | tf_op | source)
XLA Modules:
  0.0 472.9 jit_solution(7830801002838572219)
XLA Ops:
  8.0 41.2 %all-gather.5.cloned.1.call-done = bf16[1024,2048]{1,0:T(8,128)(2,1)} async-done(((bf16[128,2048]{1,0:T(8,128)(2,1)}), bf16[1024,2048]{1,0:T(8,128)(2,1)}) %all-gather.5.cloned.1.call-update) | async-done | bytes 4194320 | tf_op jit(solution)/shard_map/all_gather | solution.py:105
  49.2 5.5 %fusion.64 = bf16[4,128,1024]{2,1,0:T(8,128)(2,1)} fusion(bf16[1024,2048]{1,0:T(8,128)(2,1)} %all-gather.5.cloned.1.call-done, bf16[1,4,128,2048]{3,2,1,0:T(8,128)(2,1)S(1)} %copy-done), kind=kOutput, calls=%fused_computation.63 | convolution fusion | flops 2148007936 | bytes 7340032 | tf_op jit(solution)/shard_map/dot_general | solution.py:103
  55.0 51.8 %all-reduce.3.cloned.1.call-done = bf16[4,128,1024]{2,1,0:T(8,128)(2,1)} async-done(((bf16[4,128,1024]{2,1,0:T(8,128)(2,1)}), bf16[4,128,1024]{2,1,0:T(8,128)(2,1)}) %all-reduce.3.cloned.1.call-update) | async-done | bytes 1048592 | tf_op jit(solution)/shard_map/psum | solution.py:111
  109.3 3.7 all-to-all-start
  114.6 8.1 %all-to-all-done = bf16[8,32,1024]{2,1,0:T(8,128)(2,1)S(1)} async-done(((bf16[8,32,1024]{2,1,0:T(8,128)(2,1)}), bf16[8,32,1024]{2,1,0:T(8,128)(2,1)S(1)}, u32[]{:S(2)}, u32[]{:S(2)}) %all-to-all-start) | async-done | bytes 524320 | tf_op jit(solution)/shard_map/all_to_all | solution.py:121
  124.8 2.3 copy.83
  127.1 1.6 copy.76
  129.7 2.3 multiply_bitcast_fusion
  132.0 1.4 fusion.69
  133.3 16.1 %all-gather.7.cloned.1.call-done = bf16[4,128,1024]{2,0,1:T(4,128)(2,1)} async-done(((bf16[4,32,1024]{2,0,1:T(4,128)(2,1)}), bf16[4,128,1024]{2,0,1:T(4,128)(2,1)}) %all-gather.7.cloned.1.call-update) | async-done | bytes 1048592 | tf_op jit(solution)/shard_map/all_gather | solution.py:129
  149.5 1.5 copy.80
  151.0 1.3 fusion.88
  152.3 1.6 copy.81
  154.0 2.1 copy.82
  157.0 88.4 %while.15 = (s32[]{:T(128)}, bf16[4,128,8,128]{3,1,2,0:T(8,128)(2,1)}, f32[4,512,128]{1,2,0:T(8,128)}, bf16[4,512,128]{2,1,0:T(8,128)(2,1)}, bf16[4,128,8,128]{1...) while((s32[]{:T(128)}, ...), condition=%wide.region_6.7_spmd.clone, body=%wide.region_3.6_spmd.clone.sunk | while | flops 682891136 | bytes 27433116 | solution.py:68
  157.7 2.8 fusion.114
  160.5 2.7 fusion.116
  163.3 9.8 %fusion.117 = f32[4,512,128]{1,2,0:T(8,128)} fusion(f32[4,512,128]{1,2,0:T(8,128)} %get-tuple-element.244, s32[]{:T(128)} %get-tuple-element.242, f32[128,8,512]{2,0,1:T(8,128)} %fusion.116, bf16[4,128,8,128]{1,3,2,0:T(8,128)(2,1)} %get-tuple-element.258, f32[128,8,512]{2,0,1:T(8,128)} %get-tuple-element.228, f32[128,8]{0,1:T(8,128)S(1)} %get-tuple-element.229, ...), kind=kOutput, calls=%fused_computation.13.clone.1 | convolution fusion | flops 139986432 | bytes 8926208 | tf_op jit(solution)/shard_map/while/body/eval_jaxpr/tgl,tgd->ld/dot_general | solution.py:54
  173.1 3.1 fusion.118
  176.9 2.2 fusion.115
  179.8 2.8 fusion.114
  182.6 2.8 fusion.116
  185.4 9.8 %fusion.117 = f32[4,512,128]{1,2,0:T(8,128)} fusion(f32[4,512,128]{1,2,0:T(8,128)} %get-tuple-element.244, s32[]{:T(128)} %get-tuple-element.242, f32[128,8,512]{2,0,1:T(8,128)} %fusion.116, bf16[4,128,8,128]{1,3,2,0:T(8,128)(2,1)} %get-tuple-element.258, f32[128,8,512]{2,0,1:T(8,128)} %get-tuple-element.228, f32[128,8]{0,1:T(8,128)S(1)} %get-tuple-element.229, ...), kind=kOutput, calls=%fused_computation.13.clone.1 | convolution fusion | flops 139986432 | bytes 8926208 | tf_op jit(solution)/shard_map/while/body/eval_jaxpr/tgl,tgd->ld/dot_general | solution.py:54
  195.2 3.1 fusion.118
  199.0 2.2 fusion.115
  201.9 2.8 fusion.114
  204.7 2.7 fusion.116
  207.4 9.8 %fusion.117 = f32[4,512,128]{1,2,0:T(8,128)} fusion(f32[4,512,128]{1,2,0:T(8,128)} %get-tuple-element.244, s32[]{:T(128)} %get-tuple-element.242, f32[128,8,512]{2,0,1:T(8,128)} %fusion.116, bf16[4,128,8,128]{1,3,2,0:T(8,128)(2,1)} %get-tuple-element.258, f32[128,8,512]{2,0,1:T(8,128)} %get-tuple-element.228, f32[128,8]{0,1:T(8,128)S(1)} %get-tuple-element.229, ...), kind=kOutput, calls=%fused_computation.13.clone.1 | convolution fusion | flops 139986432 | bytes 8926208 | tf_op jit(solution)/shard_map/while/body/eval_jaxpr/tgl,tgd->ld/dot_general | solution.py:54
  217.3 3.1 fusion.118
  221.1 2.2 fusion.115
  224.0 2.8 fusion.114
  226.8 2.8 fusion.116
  229.5 9.8 %fusion.117 = f32[4,512,128]{1,2,0:T(8,128)} fusion(f32[4,512,128]{1,2,0:T(8,128)} %get-tuple-element.244, s32[]{:T(128)} %get-tuple-element.242, f32[128,8,512]{2,0,1:T(8,128)} %fusion.116, bf16[4,128,8,128]{1,3,2,0:T(8,128)(2,1)} %get-tuple-element.258, f32[128,8,512]{2,0,1:T(8,128)} %get-tuple-element.228, f32[128,8]{0,1:T(8,128)S(1)} %get-tuple-element.229, ...), kind=kOutput, calls=%fused_computation.13.clone.1 | convolution fusion | flops 139986432 | bytes 8926208 | tf_op jit(solution)/shard_map/while/body/eval_jaxpr/tgl,tgd->ld/dot_general | solution.py:54
  239.4 3.1 fusion.118
  243.2 2.2 fusion.115
  245.4 1.5 fusion.72
  249.5 1.4 copy.91
  252.0 2.1 pad_maximum_fusion
  254.2 80.2 %all-gather.9.cloned.1.call-done = bf16[4,4,128,1024]{3,2,1,0:T(8,128)(2,1)} async-done(((bf16[1,4,128,1024]{3,2,1,0:T(8,128)(2,1)}), bf16[4,4,128,1024]{3,2,1,0:T(8,128)(2,1)}) %all-gather.9.cloned.1.call-update) | async-done | bytes 4194320 | tf_op jit(solution)/shard_map/all_gather | solution.py:12
  334.4 3.3 reduce_sum.60
  338.5 13.2 %all_to_all.10 = bf16[8,32,1024]{2,1,0:T(8,128)(2,1)S(1)} all-to-all(bf16[8,32,1024]{2,1,0:T(8,128)(2,1)S(1)} %copy.93), channel_id=1, replica_groups=mesh['doc'=8,'seq'=4] {'doc'}, dimensions={0} | all-to-all | bytes 1048576 | tf_op jit(solution)/shard_map/all_to_all | solution.py:153
  353.1 24.5 %all-gather.11.cloned.1.call-done = bf16[4,128,1024]{2,0,1:T(4,128)(2,1)} async-done(((bf16[4,32,1024]{2,0,1:T(4,128)(2,1)}), bf16[4,128,1024]{2,0,1:T(4,128)(2,1)}) %all-gather.11.cloned.1.call-update) | async-done | bytes 1048592 | tf_op jit(solution)/shard_map/all_gather | solution.py:157
  377.7 1.5 copy.95
  379.2 4.4 convolution_convert_fusion
  383.6 1.9 copy.88
  385.5 1.3 broadcast_in_dim_reshape.3
  386.8 77.2 %all-reduce.5.cloned.1.call-done = bf16[1024,2048]{1,0:T(8,128)(2,1)} async-done(((bf16[1024,2048]{1,0:T(8,128)(2,1)}), bf16[1024,2048]{1,0:T(8,128)(2,1)}) %all-reduce.5.cloned.1.call-update) | async-done | bytes 4194320 | tf_op jit(solution)/shard_map/psum | solution.py:163
  463.9 2.1 dynamic-slice_convert_fusion
  (71 shorter events, 20.5 us)
Async XLA Ops:
  7.2 42.1 %copy-start = (bf16[1,4,128,2048]{3,2,1,0:T(8,128)(2,1)S(1)}, bf16[1,4,128,2048]{3,2,1,0:T(8,128)(2,1)}, u32[]{:S(2)}) copy-start(bf16[1,4,128,2048]{3,2,1,0:T(8,128)(2,1)} %param.12) | copy-start | bytes 6291460
  7.2 42.0 %all-gather.5.cloned.1.call-start = ((), (), s32[]{:S(2)}) async-start(), calls=%async_computation.2 | async-start | bytes 4718592 | tf_op jit(solution)/shard_map/all_gather | solution.py:105
  7.9 46.9 %copy-start.4 = (s32[8,4]{0,1:T(4,128)S(1)}, s32[8,4]{0,1:T(4,128)}, u32[]{:S(2)}) copy-start(s32[8,4]{0,1:T(4,128)} %param.19) | copy-start | bytes 388
  7.9 98.9 %all-reduce.3.cloned.1.call-start = ((), (), s32[]{:S(2)}) async-start(), calls=%async_computation.3 | async-start | bytes 2097152 | tf_op jit(solution)/shard_map/psum | solution.py:111
  54.7 58.3 %copy-start.7 = (s32[8]{0:T(128)S(1)}, s32[8]{0:T(128)}, u32[]{:S(2)}) copy-start(s32[8]{0:T(128)} %param.18) | copy-start | bytes 100
  54.7 59.0 %copy-start.5 = (s32[8,4]{0,1:T(4,128)S(1)}, s32[8,4]{0,1:T(4,128)}, u32[]{:S(2)}) copy-start(s32[8,4]{0,1:T(4,128)} %param.20) | copy-start | bytes 388
  107.8 16.3 %copy-start.8 = (s32[8]{0:T(128)S(1)}, s32[8]{0:T(128)}, u32[]{:S(2)}) copy-start(s32[8]{0:T(128)} %param.21) | copy-start | bytes 100
  109.3 13.4 %all-to-all-start = ((bf16[8,32,1024]{2,1,0:T(8,128)(2,1)}), bf16[8,32,1024]{2,1,0:T(8,128)(2,1)S(1)}, u32[]{:S(2)}, u32[]{:S(2)}) async-start(bf16[8,32,1024]{2,1,0:T(8,128)(2,1)} %copy.78), calls=%async_computation | async-start | bytes 1048576 | tf_op jit(solution)/shard_map/all_to_all | solution.py:121
  113.0 36.5 %all-gather.7.cloned.1.call-start = ((), (), s32[]{:S(2)}) async-start(), calls=%async_computation.4 | async-start | bytes 1310720 | tf_op jit(solution)/shard_map/all_gather | solution.py:129
  123.9 210.5 %all-gather.9.cloned.1.call-start = ((), (), s32[]{:S(2)}) async-start(), calls=%async_computation.5 | async-start | bytes 5242880 | tf_op jit(solution)/shard_map/all_gather | solution.py:12
  128.7 3.2 copy-start.6
  152.3 3.8 copy-start.3
  173.1 3.8 copy-start.1
  195.2 3.8 copy-start.1
  217.3 3.8 copy-start.1
  239.3 3.8 copy-start.1
  245.4 1.5 copy-start.2
  254.1 123.5 %all-gather.11.cloned.1.call-start = ((), (), s32[]{:S(2)}) async-start(), calls=%async_computation.6 | async-start | bytes 1310720 | tf_op jit(solution)/shard_map/all_gather | solution.py:157
  352.8 111.1 %all-reduce.5.cloned.1.call-start = ((), (), s32[]{:S(2)}) async-start(), calls=%async_computation.7 | async-start | bytes 8388608 | tf_op jit(solution)/shard_map/psum | solution.py:163
Sparse Core Ops, SparseCore 0:
  9.9 39.2 all-gather.4
  54.9 51.8 all-reduce.2
  124.0 25.4 all-gather.6
  254.2 80.1 all-gather.8
  353.0 24.6 all-gather.10
  383.7 80.1 all-reduce.4
